TPU v7x, 32 devices: a whole 2x2x4 slice. The times are simulated.
32 devices in a mesh: parts: 2 (over y), db: 4 (over z), blk: 4 (over x, core).
Axes of the slice: x: 2, y: 2, z: 4, core: 2. Of those that a mesh axis runs over, the one named last changes fastest.
Arguments:
- queries: bfloat16 [8192, 768], P(('parts', 'db', 'blk')), parts along dimension 0, may hold values from -6 to 6
- projection: bfloat16 [768, 768], replicated, may hold values from -0.21875 to 0.21875
- vectors: bfloat16 [768, 32768], P(None, ('parts', 'db', 'blk')), parts along dimension 1, may hold values from -0.21875 to 0.21875
- bins: int32 [32768], P(('parts', 'db', 'blk')), parts along dimension 0, may hold values from 0 to 127, as said below
- routes: int32 [8192, 1], P(('parts', 'db', 'blk')), parts along dimension 0, may hold values from 0 to 3; in each aligned block of 256 rows (0 to 255, 256 to 511, ...) at most 128 rows name the same one
Outputs:
- best: float32 [8192, 128], P(('parts', 'db', 'blk')), parts along dimension 0
There are 2 independent parts, one for each index of `parts`. A program takes and returns all parts, laid end to end along the dimension named above; an argument that names none is the same for every part. Nothing has to cross between parts.
Inputs may be any that keep to these rules, and one draw needn't show every extreme that they name: Within every aligned block of 1024 entries each of the 128 bins occurs exactly 1024 // 128 times. `routes`: within every aligned block of 256 rows no group is named by more than 128 rows; in every draw some block names some group exactly 128 times.
All inputs are finite; a program needn't handle non-finite values.
Results may differ from a plain program's by a relative error of at most 0.0014.
Values may be sent and summed in bfloat16 or wider, within the bound.
A program may use at most 64 MiB of HBM per device.

v0:
```python
import jax
import jax.numpy as jnp
from jax import lax
from jax.sharding import PartitionSpec as P

BINS = 128


logit_scale = 10.0


def binned_max(query_rows, columns):
    scores = jnp.dot(query_rows, columns, preferred_element_type=jnp.float32)
    return jnp.max(scores.reshape(query_rows.shape[0], -1, BINS), axis=1)


def per_device(queries, projection, vectors, bins, routes):
    groups = lax.axis_size("db")
    requests = queries.shape[0]
    capacity = 2 * requests // groups
    slab_width = vectors.shape[1]
    per_bin = slab_width // BINS
    projected = jnp.dot(queries, projection, preferred_element_type=jnp.float32)
    normed = (
        projected * lax.rsqrt(jnp.sum(projected * projected, axis=1, keepdims=True) + 1e-06)
    ).astype(jnp.bfloat16)
    target = routes[:, 0]
    one_hot = (target[:, None] == jnp.arange(groups, dtype=jnp.int32)[None, :]).astype(jnp.int32)
    slot_index = jnp.sum((jnp.cumsum(one_hot, axis=0) - one_hot) * one_hot, axis=1)
    position = target * capacity + slot_index
    chooser = (jnp.arange(groups * capacity, dtype=jnp.int32)[:, None] == position[None, :]).astype(
        jnp.bfloat16
    )
    outgoing = jnp.dot(chooser, normed, preferred_element_type=jnp.float32).astype(jnp.bfloat16)
    arrived = lax.all_to_all(outgoing, "db", split_axis=0, concat_axis=0, tiled=True)
    ordering = jnp.argsort(bins, stable=True).reshape(BINS, per_bin).T.reshape(-1)
    sorted_slab = jnp.take(vectors, ordering, axis=1)
    maxima = binned_max(arrived, lax.all_gather(sorted_slab, "blk", axis=1, tiled=True))
    answers = lax.all_to_all(logit_scale * maxima, "db", split_axis=0, concat_axis=0, tiled=True)
    return jnp.take(answers, position, axis=0)


def solution(mesh):
    in_specs = (
        P(("parts", "db", "blk"), None),
        P(),
        P(None, ("parts", "db", "blk")),
        P(("parts", "db", "blk")),
        P(("parts", "db", "blk"), None),
    )
    out_specs = P(("parts", "db", "blk"), None)
    return jax.shard_map(
        per_device, mesh=mesh, in_specs=in_specs, out_specs=out_specs, check_vma=False
    )
```

profile of v0, /device:TPU:0, one launch (start us, length us, event | category | flops | bytes accessed | tf_op | source)
XLA Modules:
  0.0 99.5 jit_solution(16236672829381784357)
XLA Ops:
  6.5 0.0 copy-start
  6.5 0.0 all-gather.2.cloned.1.call-start
  6.5 5.1 %sort.17 = (s32[1024]{0:T(1024)}, s32[1024]{0:T(1024)S(1)}) sort(s32[1024]{0:T(1024)} %param.8, s32[1024]{0:T(1024)S(1)} %iota.16), dimensions={0}, to_apply=%region_4.5 | sort | flops 10240 | bytes 16384 | tf_op jit(solution)/shard_map/jit(argsort)/sort | solution.py:36
  11.7 0.1 reshape.88
  11.9 1.7 %copy.13 = bf16[768,1024]{0,1:T(8,128)(2,1)S(1)} copy(bf16[768,1024]{1,0:T(8,128)(2,1)} %param.7) | data formatting | bytes 3145728 | tf_op args[2]
  13.6 5.2 %gather_fusion = bf16[1024,768]{1,0:T(8,128)(2,1)} fusion(bf16[768,1024]{0,1:T(8,128)(2,1)S(1)} %copy.13, s32[1024]{0:T(1024)S(1)} %broadcast_clamp_fusion), kind=kCustom, calls=%fused_computation | custom fusion | bytes 3149824 | tf_op jit(solution)/shard_map/jit(_take)/gather | solution.py:37
  18.8 2.8 %select_bitcast_fusion = bf16[768,1024]{0,1:T(8,128)(2,1)} fusion(bf16[1024,768]{1,0:T(8,128)(2,1)} %gather_fusion, pred[1024]{0:T(1024)(128)(4,1)S(1)} %compare_and_fusion), kind=kLoop, calls=%fused_computation.3 | loop fusion | flops 786432 | bytes 3146752 | tf_op jit(solution)/shard_map/jit(_take)/select_n | solution.py:37
  21.6 0.0 copy-start.2
  21.6 0.0 copy-start.1
  21.6 0.0 all-gather.2.cloned.1.call-update
  21.6 0.7 copy-done.2
  22.3 1.2 %reduce-window.6 = s32[4,2,128]{2,1,0:T(2,128)S(1)} reduce-window(s32[4,2,128]{2,1,0:T(2,128)S(1)} %compare_convert_fusion, s32[]{:T(128)} %constant.23.clone.1), window={size=1x1x128 pad=0_0x0_0x127_0}, to_apply=%region_0.0 | reduce-window | flops 130048 | bytes 8196 | tf_op jit(solution)/shard_map/reduce-window
  23.5 0.1 slice.12
  23.6 0.1 copy.9
  23.7 0.1 copy.10
  23.8 0.1 add_bitcast_fusion
  23.9 0.0 copy-done
  23.9 0.0 copy-done.1
  23.9 0.6 multiply_reduce_fusion
  24.5 0.5 convolution_convert_fusion
  25.0 26.2 %all_to_all.21 = bf16[4,128,768]{2,1,0:T(8,128)(2,1)S(1)} all-to-all(bf16[4,128,768]{2,1,0:T(8,128)(2,1)S(1)} %bitcast.46), channel_id=1, replica_groups=mesh['parts'=2,'db'=4,'blk'=4] {'db'}, dimensions={0} | all-to-all | bytes 1572864 | tf_op jit(solution)/shard_map/all_to_all | solution.py:35
  51.2 19.6 %all-gather.2.cloned.1.call-done = bf16[768,4096]{0,1:T(8,128)(2,1)} async-done(((bf16[768,1024]{0,1:T(8,128)(2,1)}), bf16[768,4096]{0,1:T(8,128)(2,1)}) %all-gather.2.cloned.1.call-update) | async-done | bytes 6291472 | tf_op jit(solution)/shard_map/all_gather | solution.py:38
  70.9 5.7 %convolution_reduce_fusion = f32[512,128]{1,0:T(8,128)S(1)} fusion(bf16[512,768,1]{1,0,2:T(8,128)(2,1)S(1)} %bitcast.47, bf16[32,128,768]{2,1,0:T(8,128)(2,1)} %bitcast.57), kind=kOutput, calls=%fused_computation.2 | convolution fusion | flops 3223257088 | bytes 7340032 | tf_op jit(solution)/shard_map/dot_general | solution.py:13
  76.5 0.7 broadcast_multiply_fusion
  77.3 4.6 %all-to-all-start.1 = ((f32[4,128,128]{2,1,0:T(8,128)}), f32[4,128,128]{2,1,0:T(8,128)S(1)}, u32[]{:S(2)}, u32[]{:S(2)}) async-start(f32[4,128,128]{2,1,0:T(8,128)} %bitcast.15), calls=%async_computation.1 | async-start | bytes 524288 | tf_op jit(solution)/shard_map/all_to_all | solution.py:39
  81.9 9.3 %all-to-all-done.1 = f32[4,128,128]{2,1,0:T(8,128)S(1)} async-done(((f32[4,128,128]{2,1,0:T(8,128)}), f32[4,128,128]{2,1,0:T(8,128)S(1)}, u32[]{:S(2)}, u32[]{:S(2)}) %all-to-all-start.1) | async-done | bytes 262176 | tf_op jit(solution)/shard_map/all_to_all | solution.py:39
  91.2 0.7 gather_fusion.1
  91.9 0.8 broadcast_select_fusion
  (13 shorter events, 0.2 us)
Async XLA Ops:
  6.5 17.4 %copy-start = (bf16[768,768]{1,0:T(8,128)(2,1)S(1)}, bf16[768,768]{1,0:T(8,128)(2,1)}, u32[]{:S(2)}) copy-start(bf16[768,768]{1,0:T(8,128)(2,1)} %param.6) | copy-start | bytes 3538948
  6.5 64.3 %all-gather.2.cloned.1.call-start = ((), (), s32[]{:S(2)}) async-start(), calls=%async_computation.2 | async-start | bytes 7864320 | tf_op jit(solution)/shard_map/all_gather | solution.py:38
  21.6 0.7 copy-start.2
  21.6 2.3 %copy-start.1 = (bf16[256,768]{1,0:T(8,128)(2,1)S(1)}, bf16[256,768]{1,0:T(8,128)(2,1)}, u32[]{:S(2)}) copy-start(bf16[256,768]{1,0:T(8,128)(2,1)} %param.5) | copy-start | bytes 1179652
  77.3 13.9 %all-to-all-start.1 = ((f32[4,128,128]{2,1,0:T(8,128)}), f32[4,128,128]{2,1,0:T(8,128)S(1)}, u32[]{:S(2)}, u32[]{:S(2)}) async-start(f32[4,128,128]{2,1,0:T(8,128)} %bitcast.15), calls=%async_computation.1 | async-start | bytes 524288 | tf_op jit(solution)/shard_map/all_to_all | solution.py:39
Sparse Core Ops, SparseCore 0:
  21.8 49.0 all-gather.1
where the time goes:
time: 99.8 us; the launch traced here: 99.5 us
  waiting for transfers between devices  29 us (29%)
  blocking collectives  26.2 us (26%)
  between operations  13.5 us (14%)
  other arithmetic  10.8 us (11%)
  local copies, waits for them, and re-layouts  8.74 us (9%)
  matrix products  6.69 us (7%)
  starting transfers between devices  4.6 us (5%)
    all_to_all x1, blocking collectives, per_device(): lax.all_to_all(outgoing, 'db', split_axis=0, concat_axis=0, tiled=True)  26.2 us
    all_gather x1, waiting for transfers between devices, per_device(): lax.all_gather(sorted_slab, 'blk', axis=1, tiled=True)  19.6 us
    all_to_all x1, waiting for transfers between devices, per_device(): lax.all_to_all(logit_scale * maxima, 'db', split_axis=0, concat_axis=0, t...  9.3 us
    dot_general x1, matrix products, binned_max(): scores = jnp.dot(query_rows, columns, preferred_element_type=jnp.float32)  5.67 us
    gather x1, local copies, waits for them, and re-layouts, per_device(): sorted_slab = jnp.take(vectors, ordering, axis=1)  5.23 us
    sort x1, other arithmetic, per_device(): jnp.argsort(bins, stable=True).reshape(BINS, per_bin).T.reshape(-1)  5.15 us
    all_to_all x1, starting transfers between devices, per_device(): lax.all_to_all(logit_scale * maxima, 'db', split_axis=0, concat_axis=0, t...  4.6 us
    select_n x2, other arithmetic, per_device(): sorted_slab = jnp.take(vectors, ordering, axis=1)  2.8 us
  transfers between devices with their start and end apart: 2, of which 2 were waited for; matrix products, arithmetic and copies ran while one was open for 3% of the time, Pallas kernels for 0%

commit v1 on v0

v1 whole, which is shorter than its diff:
```python
import functools

import jax
import jax.numpy as jnp
from jax import lax
from jax.experimental import pallas as pl
from jax.experimental.pallas import tpu as pltpu
from jax.sharding import PartitionSpec as P

BINS = 128
TILE = 256
logit_scale = 10.0
MESH = pl.DeviceIdType.MESH


def kernel(
    G, NB, C, R,
    q_hbm, p_hbm, v_hbm, bins_ref, routes_ref,
    out_ref,
    q_ref, p_ref, raw, slab, chooser, outgoing, rows, own, xout, xin, back, ans,
    load_sem, z_ss, z_rs, x_ss, x_rs, s_ss, s_rs, xb_ss, xb_rs, zb_ss, zb_rs,
):
    H = NB // 2
    n, depth = q_ref.shape
    width = raw.shape[1]
    tiles = width // TILE
    f32, bf16 = jnp.float32, jnp.bfloat16
    d = lax.axis_index("db")
    k = lax.axis_index("blk")

    loads = [
        pltpu.make_async_copy(q_hbm, q_ref, load_sem.at[0]),
        pltpu.make_async_copy(p_hbm, p_ref, load_sem.at[1]),
        pltpu.make_async_copy(v_hbm, raw, load_sem.at[2]),
    ]
    for load in loads:
        load.start()

    barrier = pltpu.get_barrier_semaphore()
    for o in range(1, G):
        pl.semaphore_signal(barrier, inc=1, device_id={"db": d ^ o}, device_id_type=MESH)
    for h in range(1, H):
        pl.semaphore_signal(barrier, inc=1, device_id={"blk": k ^ (2 * h)}, device_id_type=MESH)
    pl.semaphore_signal(barrier, inc=1, device_id={"blk": k ^ 1}, device_id_type=MESH)

    def block(c, h, o):
        return rows.at[c, pl.ds((h * G + o) * R, R)]

    def z_copy(c, o):
        return pltpu.make_async_remote_copy(
            src_ref=outgoing.at[c, pl.ds(o * R, R)], dst_ref=block(c, 0, o),
            send_sem=z_ss.at[c, o], recv_sem=z_rs.at[c, o],
            device_id={"db": d ^ o}, device_id_type=MESH)

    def x_copy(c, h, o, step):
        return pltpu.make_async_remote_copy(
            src_ref=block(c, h, o), dst_ref=block(c, h + step, o),
            send_sem=x_ss.at[c, h + step, o], recv_sem=x_rs.at[c, h + step, o],
            device_id={"blk": k ^ (2 * step)}, device_id_type=MESH)

    def s_copy(t):
        return pltpu.make_async_remote_copy(
            src_ref=slab.at[0, t], dst_ref=slab.at[1, t],
            send_sem=s_ss.at[t], recv_sem=s_rs.at[t],
            device_id={"blk": k ^ 1}, device_id_type=MESH)

    def xb_copy(c, h):
        return pltpu.make_async_remote_copy(
            src_ref=xout.at[c, h - 1], dst_ref=xin.at[c, h - 1],
            send_sem=xb_ss.at[c, h], recv_sem=xb_rs.at[c, h],
            device_id={"blk": k ^ (2 * h)}, device_id_type=MESH)

    def zb_copy(c, o):
        return pltpu.make_async_remote_copy(
            src_ref=back.at[c, pl.ds(o * R, R)], dst_ref=ans.at[c, pl.ds(o * R, R)],
            send_sem=zb_ss.at[c, o], recv_sem=zb_rs.at[c, o],
            device_id={"db": d ^ o}, device_id_type=MESH)

    started = []

    def start(copy):
        copy.start()
        started.append(copy)

    target = routes_ref[...]
    pad = max(8, G)
    hot = jnp.where(lax.broadcasted_iota(jnp.int32, (pad, n), 0) == target, 1.0, 0.0)
    before = jnp.where(
        lax.broadcasted_iota(jnp.int32, (n, n), 0) < lax.broadcasted_iota(jnp.int32, (n, n), 1),
        1.0, 0.0).astype(bf16)
    earlier = jnp.dot(hot.astype(bf16), before, preferred_element_type=f32)
    slot = jnp.sum(hot * earlier, axis=0, keepdims=True).astype(jnp.int32)
    position = (slot // R) * (G * R) + (target ^ d) * R + slot % R

    loads[0].wait()
    loads[1].wait()
    projected = jnp.dot(q_ref[...], p_ref[...], preferred_element_type=f32)
    normed = (
        projected * lax.rsqrt(jnp.sum(projected * projected, axis=1, keepdims=True) + 1e-06)
    ).astype(bf16)

    pl.semaphore_wait(barrier, G - 1 + H)

    for c in range(C):
        pick = jnp.where(
            lax.broadcasted_iota(jnp.int32, (G * R, n), 0) + c * G * R == position, 1.0, 0.0
        ).astype(bf16)
        chooser[pl.ds(c * G * R, G * R), :] = pick
        chosen = jnp.dot(pick, normed, preferred_element_type=f32).astype(bf16)
        outgoing[c] = chosen
        rows[c, pl.ds(0, R)] = chosen[:R]
        for o in range(G - 1, 0, -1):
            start(z_copy(c, o))
        if H > 1:
            start(x_copy(c, 0, 0, 1))

    loads[2].wait()
    bins = bins_ref[...]
    inner = jnp.where(
        lax.broadcasted_iota(jnp.int32, (BINS, BINS), 0)
        < lax.broadcasted_iota(jnp.int32, (BINS, BINS), 1), 1.0, 0.0).astype(bf16)
    run = jnp.zeros((BINS, 1), f32)
    places = []
    for s in range(width // BINS):
        mine = bins[:, s * BINS:(s + 1) * BINS]
        hot = jnp.where(lax.broadcasted_iota(jnp.int32, (BINS, BINS), 0) == mine, 1.0, 0.0)
        earlier = jnp.dot(hot.astype(bf16), inner, preferred_element_type=f32) + run
        rank = jnp.sum(hot * earlier, axis=0, keepdims=True).astype(jnp.int32)
        places.append(rank * BINS + mine)
        run = run + jnp.sum(hot, axis=1, keepdims=True)
    place = jnp.concatenate(places, axis=1)
    for t in range(tiles):
        move = jnp.where(
            lax.broadcasted_iota(jnp.int32, (TILE, width), 0) + t * TILE == place, 1.0, 0.0
        ).astype(bf16)
        slab[0, t] = lax.dot_general(
            raw[...], move, (((1,), (1,)), ((), ())), preferred_element_type=f32).astype(bf16)
        start(s_copy(t))

    def relay(c):
        for o in range(1, G):
            z_copy(c, o).wait_recv()
            if H > 1:
                start(x_copy(c, 0, o, 1))
        step = 2
        while step < H:
            for o in range(G):
                for h in range(step):
                    if h >= step // 2:
                        x_copy(c, h - step // 2, o, step // 2).wait_recv()
                    start(x_copy(c, h, o, step))
            step *= 2

    def score(c):
        half = H // 2
        for h in range(half, H):
            if h:
                for o in range(G):
                    x_copy(c, h - half, o, half).wait_recv()
        if c == 0:
            for t in range(tiles):
                s_copy(t).wait_recv()
        part = G * R

        for h0 in range(H):
            if H > 2 or h0 == 0:
                span = part if H > 2 else H * part
                x = rows[c, pl.ds(h0 * part, span)]
                best = None
                for side in range(2):
                    for t in range(tiles):
                        sc = jnp.dot(x, slab[side, t], preferred_element_type=f32)
                        top = jnp.maximum(sc[:, :BINS], sc[:, BINS:])
                        best = top if best is None else jnp.maximum(best, top)
                for i in range(span // part):
                    h = h0 + i
                    piece = best[i * part:(i + 1) * part]
                    if h == 0:
                        own[c] = piece
                    else:
                        xout[c, h - 1] = piece
                        start(xb_copy(c, h))

    def combine(c):
        total = own[c]
        for h in range(1, H):
            xb_copy(c, h).wait_recv()
            total = jnp.maximum(total, xin[c, h - 1])
        back[c] = total
        ans[c, pl.ds(0, R)] = total[:R]
        for o in range(G - 1, 0, -1):
            start(zb_copy(c, o))

    for step in range(C + 2):
        if step < C:
            relay(step)
        if 0 <= step - 1 < C:
            score(step - 1)
        if 0 <= step - 2 < C:
            combine(step - 2)

    total = None
    for c in range(C):
        for o in range(1, G):
            zb_copy(c, o).wait_recv()
        value = ans[c]
        high = value.astype(bf16)
        low = (value - high.astype(f32)).astype(bf16)
        got = lax.dot_general(
            chooser[pl.ds(c * G * R, G * R), :], jnp.concatenate([high, low], axis=1),
            (((0,), (0,)), ((), ())), preferred_element_type=f32)
        total = got if total is None else total + got
    out_ref[...] = total[:, :BINS] + total[:, BINS:]
    for copy in started:
        copy.wait_send()


def per_device(queries, projection, vectors, bins, routes):
    G, NB = lax.axis_size("db"), lax.axis_size("blk")
    n, depth = queries.shape
    width = vectors.shape[1]
    cap = 2 * n // G
    C = 4 if cap % 64 == 0 else 1
    R = cap // C
    H = NB // 2
    tiles = width // TILE
    f32, bf16 = jnp.float32, jnp.bfloat16
    anyspace = pl.BlockSpec(memory_space=pl.ANY)
    vmem = pl.BlockSpec(memory_space=pltpu.VMEM)
    dma = pltpu.SemaphoreType.DMA
    out = pl.pallas_call(
        functools.partial(kernel, G, NB, C, R),
        out_shape=jax.ShapeDtypeStruct((n, BINS), f32),
        in_specs=[anyspace, anyspace, anyspace, vmem, vmem],
        out_specs=vmem,
        scratch_shapes=[
            pltpu.VMEM((n, depth), bf16),
            pltpu.VMEM(projection.shape, bf16),
            pltpu.VMEM((depth, width), bf16),
            pltpu.VMEM((2, tiles, depth, TILE), bf16),
            pltpu.VMEM((C * G * R, n), bf16),
            pltpu.VMEM((C, G * R, depth), bf16),
            pltpu.VMEM((C, H * G * R, depth), bf16),
            pltpu.VMEM((C, G * R, BINS), f32),
            pltpu.VMEM((C, max(1, H - 1), G * R, BINS), f32),
            pltpu.VMEM((C, max(1, H - 1), G * R, BINS), f32),
            pltpu.VMEM((C, G * R, BINS), f32),
            pltpu.VMEM((C, G * R, BINS), f32),
            dma((3,)),
            dma((C, G)), dma((C, G)),
            dma((C, H, G)), dma((C, H, G)),
            dma((tiles,)), dma((tiles,)),
            dma((C, H)), dma((C, H)),
            dma((C, G)), dma((C, G)),
        ],
        compiler_params=pltpu.CompilerParams(
            collective_id=0, has_side_effects=True, vmem_limit_bytes=48 * 1024 * 1024),
    )(queries, projection, vectors, bins.reshape(1, -1), routes.reshape(1, -1))
    return logit_scale * out


def solution(mesh):
    in_specs = (
        P(("parts", "db", "blk"), None),
        P(),
        P(None, ("parts", "db", "blk")),
        P(("parts", "db", "blk")),
        P(("parts", "db", "blk"), None),
    )
    out_specs = P(("parts", "db", "blk"), None)
    return jax.shard_map(
        per_device, mesh=mesh, in_specs=in_specs, out_specs=out_specs, check_vma=False
    )
```

time: 99.8 us -> 48.3 us (0.48)
  Pallas kernels: 0 us -> 42.3 us
  waiting for transfers between devices: 29 us -> 0 us
  blocking collectives: 26.2 us -> 0 us
  between operations: 13.5 us -> 0.01 us
  other arithmetic: 10.8 us -> 0.67 us
  matrix products: 6.69 us -> 0 us
  starting transfers between devices: 4.6 us -> 0 us
  local copies, waits for them, and re-layouts: 8.74 us -> 5.04 us
    pallas_call x0 -> x1, Pallas kernels: none -> 42.3 us  [per_device(): pl.pallas_call(functools.partial(kernel, G, NB, C, R), out_shape=jax.Shap...]
    all_to_all x1 -> x0, blocking collectives: 26.2 us -> none  [per_device(): lax.all_to_all(outgoing, 'db', split_axis=0, concat_axis=0, tiled=True)]
    all_gather x1 -> x0, waiting for transfers between devices: 19.6 us -> none  [per_device(): lax.all_gather(sorted_slab, 'blk', axis=1, tiled=True)]
    all_to_all x1 -> x0, waiting for transfers between devices: 9.3 us -> none  [per_device(): lax.all_to_all(logit_scale * maxima, 'db', split_axis=0, concat_axis=0, t...]
    dot_general x3 -> x0, matrix products: 6.69 us -> none  [the longest x1 5.67 us: binned_max(): scores = jnp.dot(query_rows, columns, preferred_element_type=jnp.float32)]
    gather x2 -> x0, local copies, waits for them, and re-layouts: 5.96 us -> none  [the longest x1 5.23 us: per_device(): sorted_slab = jnp.take(vectors, ordering, axis=1)]
    sort x1 -> x0, other arithmetic: 5.15 us -> none  [per_device(): jnp.argsort(bins, stable=True).reshape(BINS, per_bin).T.reshape(-1)]
    all_to_all x1 -> x0, starting transfers between devices: 4.6 us -> none  [per_device(): lax.all_to_all(logit_scale * maxima, 'db', split_axis=0, concat_axis=0, t...]
  transfers between devices with their start and end apart: 2 -> 0, of which waited for: 2 -> 0; matrix products, arithmetic and copies ran while one was open for 3% -> 0% of each run, Pallas kernels for 0% -> 0%
where the time goes in v1:
time: 48.3 us; the launch traced here: 48 us
  Pallas kernels  42.3 us (88%)
  local copies, waits for them, and re-layouts  5.04 us (10%)
  other arithmetic  0.67 us (1%)
    pallas_call x1, Pallas kernels, per_device(): pl.pallas_call(functools.partial(kernel, G, NB, C, R), out_shape=jax.Shap...  42.3 us
    unnamed x10, local copies, waits for them, and re-layouts  5.04 us

profile of v1, /device:TPU:0, one launch (start us, length us, event | category | flops | bytes accessed | tf_op | source)
XLA Modules:
  0.0 48.0 jit_solution(10529419992210098663)
XLA Ops:
  0.0 0.0 copy-start
  0.0 1.4 %copy-done = bf16[768,1024]{1,0:T(8,128)(2,1)S(1)} copy-done((bf16[768,1024]{1,0:T(8,128)(2,1)S(1)}, bf16[768,1024]{1,0:T(8,128)(2,1)}, u32[]{:S(2)}) %copy-start) | copy-done | bytes 1572888
  1.4 0.0 copy-start.1
  1.4 1.3 %copy-done.1 = bf16[768,768]{1,0:T(8,128)(2,1)S(1)} copy-done((bf16[768,768]{1,0:T(8,128)(2,1)S(1)}, bf16[768,768]{1,0:T(8,128)(2,1)}, u32[]{:S(2)}) %copy-start.1) | copy-done | bytes 1179672
  2.7 0.0 copy-start.2
  2.7 1.0 %copy-done.2 = bf16[256,768]{1,0:T(8,128)(2,1)S(1)} copy-done((bf16[256,768]{1,0:T(8,128)(2,1)S(1)}, bf16[256,768]{1,0:T(8,128)(2,1)}, u32[]{:S(2)}) %copy-start.2) | copy-done | bytes 393240
  3.7 0.0 copy-start.3
  3.7 0.7 %copy-done.3 = s32[1024]{0:T(1024)S(1)} copy-done((s32[1024]{0:T(1024)S(1)}, s32[1024]{0:T(1024)}, u32[]{:S(2)}) %copy-start.3) | copy-done | bytes 4120
  4.4 0.0 copy-start.4
  4.4 0.7 %copy-done.4 = s32[256,1]{0,1:T(1,128)S(1)} copy-done((s32[256,1]{0,1:T(1,128)S(1)}, s32[256,1]{0,1:T(1,128)}, u32[]{:S(2)}) %copy-start.4) | copy-done | bytes 1048
  5.0 42.3 %shard_map.55 = f32[256,128]{1,0:T(8,128)S(1)} custom-call(bf16[256,768]{1,0:T(8,128)(2,1)S(1)} %copy-done.2, bf16[768,768]{1,0:T(8,128)(2,1)S(1)} %copy-done.1, bf16[768,1024]{1,0:T(8,128)(2,1)S(1)} %copy-done, s32[1,1024]{1,0:T(1,128)S(1)} %bitcast.2, s32[1,256]{1,0:T(1,128)S(1)} %bitcast.3), custom_call_target="tpu_custom_call" | custom-call | tf_op jit(solution)/shard_map/pallas_call | solution.py:231
  47.3 0.7 %broadcast_multiply_fusion = f32[256,128]{1,0:T(8,128)} fusion(f32[256,128]{1,0:T(8,128)S(1)} %shard_map.55), kind=kLoop, calls=%fused_computation | loop fusion | flops 32768 | bytes 262144 | tf_op jit(solution)/shard_map/mul | solution.py:259
Async XLA Ops:
  0.0 1.4 %copy-start = (bf16[768,1024]{1,0:T(8,128)(2,1)S(1)}, bf16[768,1024]{1,0:T(8,128)(2,1)}, u32[]{:S(2)}) copy-start(bf16[768,1024]{1,0:T(8,128)(2,1)} %v_hbm.1) | copy-start | bytes 4718596
  1.4 1.3 %copy-start.1 = (bf16[768,768]{1,0:T(8,128)(2,1)S(1)}, bf16[768,768]{1,0:T(8,128)(2,1)}, u32[]{:S(2)}) copy-start(bf16[768,768]{1,0:T(8,128)(2,1)} %p_hbm.1) | copy-start | bytes 3538948
  2.7 1.0 %copy-start.2 = (bf16[256,768]{1,0:T(8,128)(2,1)S(1)}, bf16[256,768]{1,0:T(8,128)(2,1)}, u32[]{:S(2)}) copy-start(bf16[256,768]{1,0:T(8,128)(2,1)} %q_hbm.1) | copy-start | bytes 1179652
  3.7 0.7 %copy-start.3 = (s32[1024]{0:T(1024)S(1)}, s32[1024]{0:T(1024)}, u32[]{:S(2)}) copy-start(s32[1024]{0:T(1024)} %param.8) | copy-start | bytes 12292
  4.4 0.7 %copy-start.4 = (s32[256,1]{0,1:T(1,128)S(1)}, s32[256,1]{0,1:T(1,128)}, u32[]{:S(2)}) copy-start(s32[256,1]{0,1:T(1,128)} %param.9) | copy-start | bytes 3076

commit v2 on v1

--- a/solution.py
+++ b/solution.py
@@ -13,11 +13,26 @@
 MESH = pl.DeviceIdType.MESH
 
 
+CODE_SCALE = 2.0 ** 26
+
+
+def encode(score):
+    scaled = score * CODE_SCALE
+    square = scaled * scaled
+    fourth = square * square
+    return jnp.where(score < 0, -fourth, fourth)
+
+
+def decode(code):
+    root = jnp.sqrt(jnp.sqrt(jnp.abs(code))) * (1.0 / CODE_SCALE)
+    return jnp.where(code < 0, -root, root)
+
+
 def kernel(
     G, NB, C, R,
-    q_hbm, p_hbm, v_hbm, bins_ref, routes_ref,
+    q_hbm, p_hbm, v_hbm, b_hbm, r_hbm,
     out_ref,
-    q_ref, p_ref, raw, slab, chooser, outgoing, rows, own, xout, xin, back, ans,
+    q_ref, p_ref, raw, bins_ref, routes_ref, slab, chooser, outgoing, rows, own, xout, xin, back, ans,
     load_sem, z_ss, z_rs, x_ss, x_rs, s_ss, s_rs, xb_ss, xb_rs, zb_ss, zb_rs,
 ):
     H = NB // 2
@@ -29,9 +44,11 @@
     k = lax.axis_index("blk")
 
     loads = [
-        pltpu.make_async_copy(q_hbm, q_ref, load_sem.at[0]),
-        pltpu.make_async_copy(p_hbm, p_ref, load_sem.at[1]),
-        pltpu.make_async_copy(v_hbm, raw, load_sem.at[2]),
+        pltpu.make_async_copy(r_hbm, routes_ref, load_sem.at[0]),
+        pltpu.make_async_copy(q_hbm, q_ref, load_sem.at[1]),
+        pltpu.make_async_copy(p_hbm, p_ref, load_sem.at[2]),
+        pltpu.make_async_copy(b_hbm, bins_ref, load_sem.at[3]),
+        pltpu.make_async_copy(v_hbm, raw, load_sem.at[4]),
     ]
     for load in loads:
         load.start()
@@ -82,6 +99,7 @@
         copy.start()
         started.append(copy)
 
+    loads[0].wait()
     target = routes_ref[...]
     pad = max(8, G)
     hot = jnp.where(lax.broadcasted_iota(jnp.int32, (pad, n), 0) == target, 1.0, 0.0)
@@ -92,8 +110,8 @@
     slot = jnp.sum(hot * earlier, axis=0, keepdims=True).astype(jnp.int32)
     position = (slot // R) * (G * R) + (target ^ d) * R + slot % R
 
-    loads[0].wait()
     loads[1].wait()
+    loads[2].wait()
     projected = jnp.dot(q_ref[...], p_ref[...], preferred_element_type=f32)
     normed = (
         projected * lax.rsqrt(jnp.sum(projected * projected, axis=1, keepdims=True) + 1e-06)
@@ -114,7 +132,8 @@
         if H > 1:
             start(x_copy(c, 0, 0, 1))
 
-    loads[2].wait()
+    loads[3].wait()
+    loads[4].wait()
     bins = bins_ref[...]
     inner = jnp.where(
         lax.broadcasted_iota(jnp.int32, (BINS, BINS), 0)
@@ -172,6 +191,7 @@
                         sc = jnp.dot(x, slab[side, t], preferred_element_type=f32)
                         top = jnp.maximum(sc[:, :BINS], sc[:, BINS:])
                         best = top if best is None else jnp.maximum(best, top)
+                best = encode(best).astype(bf16)
                 for i in range(span // part):
                     h = h0 + i
                     piece = best[i * part:(i + 1) * part]
@@ -203,14 +223,11 @@
     for c in range(C):
         for o in range(1, G):
             zb_copy(c, o).wait_recv()
-        value = ans[c]
-        high = value.astype(bf16)
-        low = (value - high.astype(f32)).astype(bf16)
         got = lax.dot_general(
-            chooser[pl.ds(c * G * R, G * R), :], jnp.concatenate([high, low], axis=1),
-            (((0,), (0,)), ((), ())), preferred_element_type=f32)
+            chooser[pl.ds(c * G * R, G * R), :], ans[c], (((0,), (0,)), ((), ())),
+            preferred_element_type=f32)
         total = got if total is None else total + got
-    out_ref[...] = total[:, :BINS] + total[:, BINS:]
+    out_ref[...] = decode(total)
     for copy in started:
         copy.wait_send()
 
@@ -225,28 +242,30 @@
     H = NB // 2
     tiles = width // TILE
     f32, bf16 = jnp.float32, jnp.bfloat16
-    anyspace = pl.BlockSpec(memory_space=pl.ANY)
+    hbm = pl.BlockSpec(memory_space=pltpu.HBM)
     vmem = pl.BlockSpec(memory_space=pltpu.VMEM)
     dma = pltpu.SemaphoreType.DMA
     out = pl.pallas_call(
         functools.partial(kernel, G, NB, C, R),
         out_shape=jax.ShapeDtypeStruct((n, BINS), f32),
-        in_specs=[anyspace, anyspace, anyspace, vmem, vmem],
+        in_specs=[hbm] * 5,
         out_specs=vmem,
         scratch_shapes=[
             pltpu.VMEM((n, depth), bf16),
             pltpu.VMEM(projection.shape, bf16),
             pltpu.VMEM((depth, width), bf16),
+            pltpu.VMEM((1, width), jnp.int32),
+            pltpu.VMEM((1, n), jnp.int32),
             pltpu.VMEM((2, tiles, depth, TILE), bf16),
             pltpu.VMEM((C * G * R, n), bf16),
             pltpu.VMEM((C, G * R, depth), bf16),
             pltpu.VMEM((C, H * G * R, depth), bf16),
-            pltpu.VMEM((C, G * R, BINS), f32),
-            pltpu.VMEM((C, max(1, H - 1), G * R, BINS), f32),
-            pltpu.VMEM((C, max(1, H - 1), G * R, BINS), f32),
-            pltpu.VMEM((C, G * R, BINS), f32),
-            pltpu.VMEM((C, G * R, BINS), f32),
-            dma((3,)),
+            pltpu.VMEM((C, G * R, BINS), bf16),
+            pltpu.VMEM((C, max(1, H - 1), G * R, BINS), bf16),
+            pltpu.VMEM((C, max(1, H - 1), G * R, BINS), bf16),
+            pltpu.VMEM((C, G * R, BINS), bf16),
+            pltpu.VMEM((C, G * R, BINS), bf16),
+            dma((5,)),
             dma((C, G)), dma((C, G)),
             dma((C, H, G)), dma((C, H, G)),
             dma((tiles,)), dma((tiles,)),
@@ -254,7 +273,7 @@
             dma((C, G)), dma((C, G)),
         ],
         compiler_params=pltpu.CompilerParams(
-            collective_id=0, has_side_effects=True, vmem_limit_bytes=48 * 1024 * 1024),
+            collective_id=0, has_side_effects=True, vmem_limit_bytes=63 * 1024 * 1024),
     )(queries, projection, vectors, bins.reshape(1, -1), routes.reshape(1, -1))
     return logit_scale * out
 

time: 48.3 us -> 42.6 us (0.88)
  local copies, waits for them, and re-layouts: 5.04 us -> 0 us
  Pallas kernels: 42.3 us -> 40.8 us
  other arithmetic: 0.67 us -> 1.57 us
    unnamed x10 -> x0, local copies, waits for them, and re-layouts: 5.04 us -> none
    pallas_call x1, Pallas kernels: 42.3 us -> 40.8 us  [per_device(): pl.pallas_call(functools.partial(kernel, G, NB, C, R), out_shape=jax.Shap...]
    mul x1, other arithmetic: 0.67 us -> 1.57 us  [per_device(): return logit_scale * out]
where the time goes in v2:
time: 42.6 us; the launch traced here: 42.4 us
  Pallas kernels  40.8 us (96%)
  other arithmetic  1.57 us (4%)
    pallas_call x1, Pallas kernels, per_device(): pl.pallas_call(functools.partial(kernel, G, NB, C, R), out_shape=jax.Shap...  40.8 us
    mul x1, other arithmetic, per_device(): return logit_scale * out  1.57 us

profile of v2, /device:TPU:0, one launch (start us, length us, event | category | flops | bytes accessed | tf_op | source)
XLA Modules:
  0.0 42.4 jit_solution(1351092894478843461)
XLA Ops:
  0.0 40.8 %shard_map.55 = f32[256,128]{1,0:T(8,128)} custom-call(bf16[256,768]{1,0:T(8,128)(2,1)} %q_hbm.1, bf16[768,768]{1,0:T(8,128)(2,1)} %p_hbm.1, bf16[768,1024]{1,0:T(8,128)(2,1)} %v_hbm.1, s32[1,1024]{1,0:T(1,128)} %bitcast.2, s32[1,256]{1,0:T(1,128)} %bitcast.3), custom_call_target="tpu_custom_call" | custom-call | tf_op jit(solution)/shard_map/pallas_call | solution.py:248
  40.8 1.6 %broadcast_multiply_fusion = f32[256,128]{1,0:T(8,128)} fusion(f32[256,128]{1,0:T(8,128)} %shard_map.55), kind=kLoop, calls=%fused_computation | loop fusion | flops 32768 | bytes 262144 | tf_op jit(solution)/shard_map/mul | solution.py:278

commit v3 on v2

--- a/solution.py
+++ b/solution.py
@@ -29,13 +29,15 @@
 
 
 def kernel(
-    G, NB, C, R,
+    G, NB, sizes,
     q_hbm, p_hbm, v_hbm, b_hbm, r_hbm,
     out_ref,
     q_ref, p_ref, raw, bins_ref, routes_ref, slab, chooser, outgoing, rows, own, xout, xin, back, ans,
     load_sem, z_ss, z_rs, x_ss, x_rs, s_ss, s_rs, xb_ss, xb_rs, zb_ss, zb_rs,
 ):
     H = NB // 2
+    C = len(sizes)
+    firsts = [sum(sizes[:c]) for c in range(C)]
     n, depth = q_ref.shape
     width = raw.shape[1]
     tiles = width // TILE
@@ -61,11 +63,17 @@
     pl.semaphore_signal(barrier, inc=1, device_id={"blk": k ^ 1}, device_id_type=MESH)
 
     def block(c, h, o):
-        return rows.at[c, pl.ds((h * G + o) * R, R)]
+        return rows.at[pl.ds(H * G * firsts[c] + (h * G + o) * sizes[c], sizes[c])]
+
+    def part(c, o):
+        return pl.ds(G * firsts[c] + o * sizes[c], sizes[c])
+
+    def whole(c):
+        return pl.ds(G * firsts[c], G * sizes[c])
 
     def z_copy(c, o):
         return pltpu.make_async_remote_copy(
-            src_ref=outgoing.at[c, pl.ds(o * R, R)], dst_ref=block(c, 0, o),
+            src_ref=outgoing.at[part(c, o)], dst_ref=block(c, 0, o),
             send_sem=z_ss.at[c, o], recv_sem=z_rs.at[c, o],
             device_id={"db": d ^ o}, device_id_type=MESH)
 
@@ -83,13 +91,13 @@
 
     def xb_copy(c, h):
         return pltpu.make_async_remote_copy(
-            src_ref=xout.at[c, h - 1], dst_ref=xin.at[c, h - 1],
+            src_ref=xout.at[h - 1, whole(c)], dst_ref=xin.at[h - 1, whole(c)],
             send_sem=xb_ss.at[c, h], recv_sem=xb_rs.at[c, h],
             device_id={"blk": k ^ (2 * h)}, device_id_type=MESH)
 
     def zb_copy(c, o):
         return pltpu.make_async_remote_copy(
-            src_ref=back.at[c, pl.ds(o * R, R)], dst_ref=ans.at[c, pl.ds(o * R, R)],
+            src_ref=back.at[part(c, o)], dst_ref=ans.at[part(c, o)],
             send_sem=zb_ss.at[c, o], recv_sem=zb_rs.at[c, o],
             device_id={"db": d ^ o}, device_id_type=MESH)
 
@@ -108,7 +116,11 @@
         1.0, 0.0).astype(bf16)
     earlier = jnp.dot(hot.astype(bf16), before, preferred_element_type=f32)
     slot = jnp.sum(hot * earlier, axis=0, keepdims=True).astype(jnp.int32)
-    position = (slot // R) * (G * R) + (target ^ d) * R + slot % R
+    position = (target ^ d) * sizes[0] + slot
+    for c in range(1, C):
+        position = jnp.where(
+            slot < firsts[c], position,
+            G * firsts[c] + (target ^ d) * sizes[c] + slot - firsts[c])
 
     loads[1].wait()
     loads[2].wait()
@@ -121,13 +133,13 @@
 
     for c in range(C):
         pick = jnp.where(
-            lax.broadcasted_iota(jnp.int32, (G * R, n), 0) + c * G * R == position, 1.0, 0.0
-        ).astype(bf16)
-        chooser[pl.ds(c * G * R, G * R), :] = pick
+            lax.broadcasted_iota(jnp.int32, (G * sizes[c], n), 0) + G * firsts[c] == position,
+            1.0, 0.0).astype(bf16)
+        chooser[whole(c), :] = pick
         chosen = jnp.dot(pick, normed, preferred_element_type=f32).astype(bf16)
-        outgoing[c] = chosen
-        rows[c, pl.ds(0, R)] = chosen[:R]
-        for o in range(G - 1, 0, -1):
+        outgoing[whole(c)] = chosen
+        rows[pl.ds(H * G * firsts[c], sizes[c])] = chosen[:sizes[c]]
+        for o in range(1, G):
             start(z_copy(c, o))
         if H > 1:
             start(x_copy(c, 0, 0, 1))
@@ -179,12 +191,13 @@
         if c == 0:
             for t in range(tiles):
                 s_copy(t).wait_recv()
-        part = G * R
+        count = G * sizes[c]
+        base = H * G * firsts[c]
 
         for h0 in range(H):
             if H > 2 or h0 == 0:
-                span = part if H > 2 else H * part
-                x = rows[c, pl.ds(h0 * part, span)]
+                span = count if H > 2 else H * count
+                x = rows[pl.ds(base + h0 * count, span)]
                 best = None
                 for side in range(2):
                     for t in range(tiles):
@@ -192,22 +205,22 @@
                         top = jnp.maximum(sc[:, :BINS], sc[:, BINS:])
                         best = top if best is None else jnp.maximum(best, top)
                 best = encode(best).astype(bf16)
-                for i in range(span // part):
+                for i in range(span // count):
                     h = h0 + i
-                    piece = best[i * part:(i + 1) * part]
+                    piece = best[i * count:(i + 1) * count]
                     if h == 0:
-                        own[c] = piece
+                        own[whole(c)] = piece
                     else:
-                        xout[c, h - 1] = piece
+                        xout[h - 1, whole(c)] = piece
                         start(xb_copy(c, h))
 
     def combine(c):
-        total = own[c]
+        total = own[whole(c)]
         for h in range(1, H):
             xb_copy(c, h).wait_recv()
-            total = jnp.maximum(total, xin[c, h - 1])
-        back[c] = total
-        ans[c, pl.ds(0, R)] = total[:R]
+            total = jnp.maximum(total, xin[h - 1, whole(c)])
+        back[whole(c)] = total
+        ans[part(c, 0)] = total[:sizes[c]]
         for o in range(G - 1, 0, -1):
             start(zb_copy(c, o))
 
@@ -224,7 +237,7 @@
         for o in range(1, G):
             zb_copy(c, o).wait_recv()
         got = lax.dot_general(
-            chooser[pl.ds(c * G * R, G * R), :], ans[c], (((0,), (0,)), ((), ())),
+            chooser[whole(c), :], ans[whole(c)], (((0,), (0,)), ((), ())),
             preferred_element_type=f32)
         total = got if total is None else total + got
     out_ref[...] = decode(total)
@@ -237,8 +250,9 @@
     n, depth = queries.shape
     width = vectors.shape[1]
     cap = 2 * n // G
-    C = 4 if cap % 64 == 0 else 1
-    R = cap // C
+    unit = cap // 8
+    sizes = [3 * unit, 3 * unit, 2 * unit] if cap % 128 == 0 else [cap]
+    C = len(sizes)
     H = NB // 2
     tiles = width // TILE
     f32, bf16 = jnp.float32, jnp.bfloat16
@@ -246,7 +260,7 @@
     vmem = pl.BlockSpec(memory_space=pltpu.VMEM)
     dma = pltpu.SemaphoreType.DMA
     out = pl.pallas_call(
-        functools.partial(kernel, G, NB, C, R),
+        functools.partial(kernel, G, NB, tuple(sizes)),
         out_shape=jax.ShapeDtypeStruct((n, BINS), f32),
         in_specs=[hbm] * 5,
         out_specs=vmem,
@@ -257,14 +271,14 @@
             pltpu.VMEM((1, width), jnp.int32),
             pltpu.VMEM((1, n), jnp.int32),
             pltpu.VMEM((2, tiles, depth, TILE), bf16),
-            pltpu.VMEM((C * G * R, n), bf16),
-            pltpu.VMEM((C, G * R, depth), bf16),
-            pltpu.VMEM((C, H * G * R, depth), bf16),
-            pltpu.VMEM((C, G * R, BINS), bf16),
-            pltpu.VMEM((C, max(1, H - 1), G * R, BINS), bf16),
-            pltpu.VMEM((C, max(1, H - 1), G * R, BINS), bf16),
-            pltpu.VMEM((C, G * R, BINS), bf16),
-            pltpu.VMEM((C, G * R, BINS), bf16),
+            pltpu.VMEM((G * cap, n), bf16),
+            pltpu.VMEM((G * cap, depth), bf16),
+            pltpu.VMEM((H * G * cap, depth), bf16),
+            pltpu.VMEM((G * cap, BINS), bf16),
+            pltpu.VMEM((max(1, H - 1), G * cap, BINS), bf16),
+            pltpu.VMEM((max(1, H - 1), G * cap, BINS), bf16),
+            pltpu.VMEM((G * cap, BINS), bf16),
+            pltpu.VMEM((G * cap, BINS), bf16),
             dma((5,)),
             dma((C, G)), dma((C, G)),
             dma((C, H, G)), dma((C, H, G)),

time: 42.6 us -> 39.8 us (0.934)
  Pallas kernels: 40.8 us -> 38.1 us
    pallas_call x1, Pallas kernels: 40.8 us -> 38.1 us  [per_device(): pl.pallas_call(functools.partial(kernel, G, NB, tuple(sizes)), out_shape=...]
where the time goes in v3:
time: 39.8 us; the launch traced here: 39.7 us
  Pallas kernels  38.1 us (96%)
  other arithmetic  1.57 us (4%)
    pallas_call x1, Pallas kernels, per_device(): pl.pallas_call(functools.partial(kernel, G, NB, tuple(sizes)), out_shape=...  38.1 us
    mul x1, other arithmetic, per_device(): return logit_scale * out  1.57 us

profile of v3, /device:TPU:0, one launch (start us, length us, event | category | flops | bytes accessed | tf_op | source)
XLA Modules:
  0.0 39.7 jit_solution(5850985094446855172)
XLA Ops:
  0.0 38.1 %shard_map.55 = f32[256,128]{1,0:T(8,128)} custom-call(bf16[256,768]{1,0:T(8,128)(2,1)} %q_hbm.1, bf16[768,768]{1,0:T(8,128)(2,1)} %p_hbm.1, bf16[768,1024]{1,0:T(8,128)(2,1)} %v_hbm.1, s32[1,1024]{1,0:T(1,128)} %bitcast.2, s32[1,256]{1,0:T(1,128)} %bitcast.3), custom_call_target="tpu_custom_call" | custom-call | tf_op jit(solution)/shard_map/pallas_call | solution.py:262
  38.1 1.6 %broadcast_multiply_fusion = f32[256,128]{1,0:T(8,128)} fusion(f32[256,128]{1,0:T(8,128)} %shard_map.55), kind=kLoop, calls=%fused_computation | loop fusion | flops 32768 | bytes 262144 | tf_op jit(solution)/shard_map/mul | solution.py:292
